TPU v7x, 512 devices: a whole 4x4x16 slice. The times are simulated.
512 devices in a mesh: dp: 64 (over x, z), ctx: 8 (over y, core).
Axes of the slice: x: 4, y: 4, z: 16, core: 2. Of those that a mesh axis runs over, the one named last changes fastest.
Arguments:
- projections: bfloat16 [131072, 6144], P(('dp', 'ctx')), may hold values from -6 to 6
- block_source: int32 [64, 8, 2], P('dp', 'ctx'), may hold values from 0 to 1023, as said below
- clip_ids: int32 [64, 16], P('dp'), may hold values from 0 to 8, as said below
- out_weight: bfloat16 [2048, 1536], P('dp'), may hold values from -1 to 1
Outputs:
- mixed: bfloat16 [131072, 1536], P(('dp', 'ctx'))
Inputs may be any that keep to these rules, and one draw needn't show every extreme that they name: `block_source`: arrival block a lies on the device numbered a // 2 in dp-major order (dp index a // (2 * 8), ctx index (a // 2) % 8). The block that fills pack block (o, j, l) lies on the device with the same ctx index j and dp index o or o XOR 1. Every arrival block fills exactly one pack block. `clip_ids`: in each pack the clip numbers start at 0, never fall and rise by at most one from block to block; every clip spans 1 to 8 blocks, and in every pack some clip spans exactly 8 blocks.
All inputs are finite; a program needn't handle non-finite values.
Results may differ from a plain program's by a relative error of at most 0.0057.
Values may be sent and summed in bfloat16 or wider, within the bound.
A program may use at most 64 MiB of HBM per device.

v0:
```python
import math
import jax
import jax.numpy as jnp
from jax import lax
from jax.sharding import PartitionSpec as P

HEAD = 128
big_negative = -1e30


def partner(value, axis, bit):
    mask = 2**bit
    pairs = [(source, source ^ mask) for source in range(lax.axis_size(axis))]
    return lax.ppermute(value, axis, pairs)


def soft_weights(scores, allowed):
    masked = jnp.where(allowed, scores, big_negative)
    row_max = jnp.max(masked, axis=-1, keepdims=True)
    exponent = jnp.exp(masked - row_max)
    return (exponent / jnp.sum(exponent, axis=-1, keepdims=True)).astype(jnp.bfloat16)


def attend_dense(queries, key_rows, value_rows, token_clip, scaling):
    token_count, head_count, head_size = queries.shape
    step_size = min(token_count, 512)
    step_count = token_count // step_size
    query_steps = queries.reshape(step_count, step_size, head_count, head_size)
    clip_steps = token_clip.reshape(step_count, step_size)

    def one_step(arguments):
        query_block, clip_block = arguments
        scores = (
            jnp.einsum("qhe,khe->hqk", query_block, key_rows, preferred_element_type=jnp.float32)
            * scaling
        )
        allowed = (clip_block[:, None] == token_clip[None, :])[None]
        weights = soft_weights(scores, allowed)
        return jnp.einsum(
            "hqk,khe->qhe", weights, value_rows, preferred_element_type=jnp.float32
        ).astype(jnp.bfloat16)

    outputs = lax.map(one_step, (query_steps, clip_steps))
    return outputs.reshape(token_count, head_count, head_size)


def body(projections, block_source, clip_ids, out_weight):
    ctx_count = lax.axis_size("ctx")
    local_rows, row_width = projections.shape
    local_blocks = block_source.shape[2]
    block_rows = local_rows // local_blocks
    own_blocks = projections.reshape(local_blocks, block_rows, row_width)
    partner_blocks = partner(own_blocks, "dp", 0)
    source_ids = block_source.reshape(local_blocks)
    from_partner = source_ids // (local_blocks * ctx_count) != lax.axis_index("dp")
    chosen_slot = source_ids % local_blocks + local_blocks * from_partner.astype(jnp.int32)
    candidates = jnp.concatenate([own_blocks, partner_blocks], axis=0)
    packed = jnp.take(candidates, chosen_slot, axis=0)
    local_heads = row_width // (3 * HEAD) // ctx_count
    grouped = packed.reshape(local_rows, ctx_count, local_heads, 3 * HEAD)
    block_clip = clip_ids.reshape(-1)
    token_clip = jnp.repeat(block_clip, block_rows)
    scaling = 1.0 / math.sqrt(HEAD)
    regrouped = lax.all_to_all(grouped, "ctx", split_axis=1, concat_axis=0, tiled=True)
    token_count = regrouped.shape[0]
    item_count = regrouped.shape[2]
    features = regrouped.reshape(token_count, item_count, 3 * HEAD)
    queries = features[:, :, :HEAD]
    key_rows = features[:, :, HEAD : 2 * HEAD]
    value_rows = features[:, :, 2 * HEAD :]
    attended = attend_dense(queries, key_rows, value_rows, token_clip, scaling)
    merged = attended.reshape(local_rows * ctx_count, local_heads * HEAD)
    attention_rows = lax.all_to_all(merged, "ctx", split_axis=0, concat_axis=1, tiled=True)
    result = jnp.dot(
        attention_rows,
        lax.all_gather(out_weight, "dp", axis=0, tiled=True),
        preferred_element_type=jnp.float32,
    )
    return result.astype(jnp.bfloat16)


def solution(mesh):
    return jax.shard_map(
        body,
        mesh=mesh,
        in_specs=(P(("dp", "ctx"), None), P("dp", "ctx", None), P("dp", None), P("dp", None)),
        out_specs=P(("dp", "ctx"), None),
        check_vma=False,
    )
```

profile of v0, /device:TPU:8, one launch (start us, length us, event | category | flops | bytes accessed | tf_op | source)
XLA Modules:
  0.0 276.1 jit_solution(7214846663131477792)
XLA Ops:
  6.5 3.8 %collective-permute-start = (bf16[2,128,6144]{2,1,0:T(8,128)(2,1)}, bf16[2,128,6144]{2,1,0:T(8,128)(2,1)S(1)}, u32[]{:S(2)}, u32[]{:S(2)}) collective-permute-start(bf16[2,128,6144]{2,1,0:T(8,128)(2,1)} %bitcast.87), channel_id=1, source_target_pairs={{0,8},{8,0},{16,24},{24,16},{32,40},{40,32},{48,56},{56,48},{64,72... | collective-permute-start | bytes 9437192 | tf_op jit(solution)/shard_map/ppermute | solution.py:14
  10.4 0.7 fusion.31
  11.0 0.7 compare_and_fusion
  11.7 0.1 broadcast_bitcast_fusion.2
  11.8 66.9 %collective-permute-done = bf16[2,128,6144]{2,1,0:T(8,128)(2,1)S(1)} collective-permute-done((bf16[2,128,6144]{2,1,0:T(8,128)(2,1)}, bf16[2,128,6144]{2,1,0:T(8,128)(2,1)S(1)}, u32[]{:S(2)}, u32[]{:S(2)}) %collective-permute-start) | collective-permute-done | bytes 3145760 | tf_op jit(solution)/shard_map/ppermute | solution.py:14
  78.7 5.1 %pad_maximum_fusion = bf16[4,128,6144]{2,1,0:T(8,128)(2,1)} fusion(bf16[2,128,6144]{2,1,0:T(8,128)(2,1)S(1)} %collective-permute-done, bf16[2,128,6144]{2,1,0:T(8,128)(2,1)} %bitcast.88), kind=kLoop, calls=%fused_computation.27 | loop fusion | flops 3145728 | bytes 12582912 | tf_op jit(solution)/shard_map/concatenate | solution.py:57
  83.7 3.5 %gather_fusion = bf16[2,128,6144]{2,1,0:T(8,128)(2,1)S(1)} fusion(bf16[4,128,6144]{2,1,0:T(8,128)(2,1)} %pad_maximum_fusion, s32[1024]{0:T(1024)S(1)} %pad_clamp_fusion), kind=kCustom, calls=%fused_computation | custom fusion | bytes 6291464 | tf_op jit(solution)/shard_map/jit(_take)/gather | solution.py:58
  87.3 3.5 %gather.7 = bf16[256,8,2,384]{3,2,1,0:T(2,128)(2,1)} reshape(bf16[2,128,6144]{2,1,0:T(8,128)(2,1)S(1)} %gather_fusion) | data formatting | bytes 6291456 | tf_op jit(solution)/shard_map/jit(_take)/gather | solution.py:58
  90.8 5.0 %broadcast_select_fusion = bf16[256,8,2,384]{3,2,1,0:T(2,128)(2,1)S(1)} fusion(bf16[256,8,2,384]{3,2,1,0:T(2,128)(2,1)} %gather.7, pred[256]{0:T(512)(128)(4,1)S(1)} %broadcast_bitcast_fusion.2), kind=kLoop, calls=%fused_computation.28 | loop fusion | flops 1572864 | bytes 6291712 | tf_op jit(solution)/shard_map/jit(_take)/select_n | solution.py:58
  95.8 4.1 %copy.12 = bf16[256,8,2,384]{3,2,0,1:T(2,128)(2,1)} copy(bf16[256,8,2,384]{3,2,1,0:T(2,128)(2,1)S(1)} %broadcast_select_fusion) | data formatting | bytes 6291456 | tf_op jit(solution)/shard_map/jit(_take)/select_n | solution.py:58
  99.9 5.0 %all-to-all-start = ((bf16[256,8,2,384]{3,2,0,1:T(2,128)(2,1)}), bf16[256,8,2,384]{3,2,0,1:T(2,128)(2,1)S(1)}, u32[]{:S(2)}, u32[]{:S(2)}) async-start(bf16[256,8,2,384]{3,2,0,1:T(2,128)(2,1)} %copy.12), calls=%async_computation | async-start | bytes 6291456 | tf_op jit(solution)/shard_map/all_to_all | solution.py:64
  104.9 0.0 all-gather.2.cloned.1.call-start
  104.9 0.7 all-gather.2.cloned.1.call-update
  105.6 0.5 broadcast.219
  106.1 0.0 copy-done.1
  106.1 0.6 reduce.3
  106.7 0.1 broadcast_in_dim.47
  106.8 0.1 broadcast_bitcast_fusion.1
  106.9 35.0 %all-to-all-done = bf16[256,8,2,384]{3,2,0,1:T(2,128)(2,1)S(1)} async-done(((bf16[256,8,2,384]{3,2,0,1:T(2,128)(2,1)}), bf16[256,8,2,384]{3,2,0,1:T(2,128)(2,1)S(1)}, u32[]{:S(2)}, u32[]{:S(2)}) %all-to-all-start) | async-done | bytes 3145760 | tf_op jit(solution)/shard_map/all_to_all | solution.py:64
  141.9 0.6 copy.13
  142.4 0.0 copy-start
  142.5 1.9 fusion.37
  144.3 53.7 %while.11 = (s32[]{:T(128)}, bf16[4,512,2,128]{3,2,1,0:T(2,128)(2,1)S(1)}, s32[4,512]{1,0:T(4,128)S(1)}, bf16[4,512,2,128]{3,1,0,2:T(8,128)(2,1)}, bf16[2048,2,1...) while((s32[]{:T(128)}, ...), condition=%wide.region_3.4_spmd.clone, body=%wide.region_0.3_spmd.clone.sunk | while | flops 1087506432 | bytes 22051484 | solution.py:43
  144.3 0.1 broadcast_bitcast_fusion.4
  144.4 0.7 broadcast_compare_fusion.2
  145.1 7.7 %fusion.51 = (f32[2,512]{1,0:T(2,128)S(1)}, f32[2,512,2048]{2,1,0:T(8,128)}) fusion(pred[512,2048]{1,0:T(8,128)(4,1)S(1)} %broadcast_compare_fusion.2, bf16[2048,2,128]{2,0,1:T(8,128)(2,1)} %get-tuple-element.167, bf16[4,512,2,128]{3,1,0,2:T(8,128)(2,1)} %get-tuple-element.166, s32[]{:T(128)} %get-tuple-element.155), kind=kOutput, calls=%fused_computation.56.clone.1 | convolution fusion | flops 545261568 | bytes 10752512 | tf_op jit(solution)/shard_map/while/body/eval_jaxpr/sub | solution.py:20
  152.7 4.7 %fusion.52 = bf16[1,512,2,128]{3,1,2,0:T(8,128)(2,1)S(1)} fusion(bf16[2048,2,128]{2,0,1:T(8,128)(2,1)S(1)} %get-tuple-element.168, f32[2,512,2048]{2,1,0:T(8,128)} %get-tuple-element.145, f32[2,512]{1,0:T(2,128)S(1)} %get-tuple-element.146), kind=kOutput, calls=%fused_computation.13.clone.1 | convolution fusion | flops 541196288 | bytes 9703424 | tf_op jit(solution)/shard_map/while/body/eval_jaxpr/hqk,khe->qhe/dot_general | solution.py:39
  157.4 0.3 copy_dynamic-update-slice_fusion.2
  157.8 0.1 broadcast_bitcast_fusion.4
  157.8 0.7 broadcast_compare_fusion.2
  158.5 7.7 %fusion.51 = (f32[2,512]{1,0:T(2,128)S(1)}, f32[2,512,2048]{2,1,0:T(8,128)}) fusion(pred[512,2048]{1,0:T(8,128)(4,1)S(1)} %broadcast_compare_fusion.2, bf16[2048,2,128]{2,0,1:T(8,128)(2,1)} %get-tuple-element.167, bf16[4,512,2,128]{3,1,0,2:T(8,128)(2,1)} %get-tuple-element.166, s32[]{:T(128)} %get-tuple-element.155), kind=kOutput, calls=%fused_computation.56.clone.1 | convolution fusion | flops 545261568 | bytes 10752512 | tf_op jit(solution)/shard_map/while/body/eval_jaxpr/sub | solution.py:20
  166.2 4.7 %fusion.52 = bf16[1,512,2,128]{3,1,2,0:T(8,128)(2,1)S(1)} fusion(bf16[2048,2,128]{2,0,1:T(8,128)(2,1)S(1)} %get-tuple-element.168, f32[2,512,2048]{2,1,0:T(8,128)} %get-tuple-element.145, f32[2,512]{1,0:T(2,128)S(1)} %get-tuple-element.146), kind=kOutput, calls=%fused_computation.13.clone.1 | convolution fusion | flops 541196288 | bytes 9703424 | tf_op jit(solution)/shard_map/while/body/eval_jaxpr/hqk,khe->qhe/dot_general | solution.py:39
  170.9 0.3 copy_dynamic-update-slice_fusion.2
  171.2 0.1 broadcast_bitcast_fusion.4
  171.3 0.7 broadcast_compare_fusion.2
  171.9 7.7 %fusion.51 = (f32[2,512]{1,0:T(2,128)S(1)}, f32[2,512,2048]{2,1,0:T(8,128)}) fusion(pred[512,2048]{1,0:T(8,128)(4,1)S(1)} %broadcast_compare_fusion.2, bf16[2048,2,128]{2,0,1:T(8,128)(2,1)} %get-tuple-element.167, bf16[4,512,2,128]{3,1,0,2:T(8,128)(2,1)} %get-tuple-element.166, s32[]{:T(128)} %get-tuple-element.155), kind=kOutput, calls=%fused_computation.56.clone.1 | convolution fusion | flops 545261568 | bytes 10752512 | tf_op jit(solution)/shard_map/while/body/eval_jaxpr/sub | solution.py:20
  179.6 4.7 %fusion.52 = bf16[1,512,2,128]{3,1,2,0:T(8,128)(2,1)S(1)} fusion(bf16[2048,2,128]{2,0,1:T(8,128)(2,1)S(1)} %get-tuple-element.168, f32[2,512,2048]{2,1,0:T(8,128)} %get-tuple-element.145, f32[2,512]{1,0:T(2,128)S(1)} %get-tuple-element.146), kind=kOutput, calls=%fused_computation.13.clone.1 | convolution fusion | flops 541196288 | bytes 9703424 | tf_op jit(solution)/shard_map/while/body/eval_jaxpr/hqk,khe->qhe/dot_general | solution.py:39
  184.3 0.3 copy_dynamic-update-slice_fusion.2
  184.6 0.1 broadcast_bitcast_fusion.4
  184.7 0.7 broadcast_compare_fusion.2
  185.3 7.7 %fusion.51 = (f32[2,512]{1,0:T(2,128)S(1)}, f32[2,512,2048]{2,1,0:T(8,128)}) fusion(pred[512,2048]{1,0:T(8,128)(4,1)S(1)} %broadcast_compare_fusion.2, bf16[2048,2,128]{2,0,1:T(8,128)(2,1)} %get-tuple-element.167, bf16[4,512,2,128]{3,1,0,2:T(8,128)(2,1)} %get-tuple-element.166, s32[]{:T(128)} %get-tuple-element.155), kind=kOutput, calls=%fused_computation.56.clone.1 | convolution fusion | flops 545261568 | bytes 10752512 | tf_op jit(solution)/shard_map/while/body/eval_jaxpr/sub | solution.py:20
  193.0 4.7 %fusion.52 = bf16[1,512,2,128]{3,1,2,0:T(8,128)(2,1)S(1)} fusion(bf16[2048,2,128]{2,0,1:T(8,128)(2,1)S(1)} %get-tuple-element.168, f32[2,512,2048]{2,1,0:T(8,128)} %get-tuple-element.145, f32[2,512]{1,0:T(2,128)S(1)} %get-tuple-element.146), kind=kOutput, calls=%fused_computation.13.clone.1 | convolution fusion | flops 541196288 | bytes 9703424 | tf_op jit(solution)/shard_map/while/body/eval_jaxpr/hqk,khe->qhe/dot_general | solution.py:39
  197.7 0.3 copy_dynamic-update-slice_fusion.2
  198.0 0.7 all_to_all.28
  198.7 18.5 %all_to_all.34 = bf16[8,256,256]{2,1,0:T(8,128)(2,1)S(1)} all-to-all(bf16[8,256,256]{2,1,0:T(8,128)(2,1)S(1)} %all_to_all.28), channel_id=1, replica_groups=mesh['dp'=64,'ctx'=8] {'ctx'}, dimensions={0} | all-to-all | bytes 2097152 | tf_op jit(solution)/shard_map/all_to_all | solution.py:73
  217.2 0.5 copy.16
  217.7 46.0 %all-gather.2.cloned.1.call-done = bf16[2048,1536]{1,0:T(8,128)(2,1)} async-done(((bf16[32,1536]{1,0:T(8,128)(2,1)}), bf16[2048,1536]{1,0:T(8,128)(2,1)}) %all-gather.2.cloned.1.call-update) | async-done | bytes 6291472 | tf_op jit(solution)/shard_map/all_gather | solution.py:76
  263.7 5.5 %convolution_convert_fusion = bf16[256,1536]{1,0:T(8,128)(2,1)} fusion(bf16[256,2048]{0,1:T(8,128)(2,1)S(1)} %bitcast.85, bf16[2048,1536]{1,0:T(8,128)(2,1)} %all-gather.2.cloned.1.call-done), kind=kOutput, calls=%fused_computation.29 | convolution fusion | flops 1611005952 | bytes 8126464 | tf_op jit(solution)/shard_map/dot_general | solution.py:74
  (9 shorter events, 0.0 us)
Async XLA Ops:
  6.5 72.1 %collective-permute-start = (bf16[2,128,6144]{2,1,0:T(8,128)(2,1)}, bf16[2,128,6144]{2,1,0:T(8,128)(2,1)S(1)}, u32[]{:S(2)}, u32[]{:S(2)}) collective-permute-start(bf16[2,128,6144]{2,1,0:T(8,128)(2,1)} %bitcast.87), channel_id=1, source_target_pairs={{0,8},{8,0},{16,24},{24,16},{32,40},{40,32},{48,56},{56,48},{64,72... | collective-permute-start | bytes 9437192 | tf_op jit(solution)/shard_map/ppermute | solution.py:14
  99.9 6.3 %copy-start.1 = (s32[1,16]{1,0:T(1,128)S(1)}, s32[1,16]{1,0:T(1,128)}, u32[]{:S(2)}) copy-start(s32[1,16]{1,0:T(1,128)} %param.8) | copy-start | bytes 196
  99.9 42.0 %all-to-all-start = ((bf16[256,8,2,384]{3,2,0,1:T(2,128)(2,1)}), bf16[256,8,2,384]{3,2,0,1:T(2,128)(2,1)S(1)}, u32[]{:S(2)}, u32[]{:S(2)}) async-start(bf16[256,8,2,384]{3,2,0,1:T(2,128)(2,1)} %copy.12), calls=%async_computation | async-start | bytes 6291456 | tf_op jit(solution)/shard_map/all_to_all | solution.py:64
  104.9 158.8 %all-gather.2.cloned.1.call-start = ((), (), s32[]{:S(2)}) async-start(), calls=%async_computation.2 | async-start | bytes 6389760 | tf_op jit(solution)/shard_map/all_gather | solution.py:76
  142.4 1.9 copy-start
Sparse Core Ops, SparseCore 0:
  108.7 155.0 all-gather.1
where the time goes:
time: 277 us; the launch traced here: 276 us
  waiting for transfers between devices  149 us (54%)
  matrix products  54.9 us (20%)
  blocking collectives  18.5 us (7%)
  local copies, waits for them, and re-layouts  17.1 us (6%)
  other arithmetic  14.6 us (5%)
  between operations  13.5 us (5%)
  starting transfers between devices  8.87 us (3%)
    ppermute x1, waiting for transfers between devices, partner(): return lax.ppermute(value, axis, pairs)  66.9 us
    all_gather x1, waiting for transfers between devices, body(): lax.all_gather(out_weight, 'dp', axis=0, tiled=True)  46 us
    all_to_all x1, waiting for transfers between devices, body(): lax.all_to_all(grouped, 'ctx', split_axis=1, concat_axis=0, tiled=True)  35 us
    sub x4, matrix products, soft_weights(): exponent = jnp.exp(masked - row_max)  30.7 us
    dot_general x4, matrix products, one_step(): jnp.einsum('hqk,khe->qhe', weights, value_rows, preferred_element_type=jn...  18.7 us
    all_to_all x1, blocking collectives, body(): lax.all_to_all(merged, 'ctx', split_axis=0, concat_axis=1, tiled=True)  18.5 us
    gather x2, local copies, waits for them, and re-layouts, body(): packed = jnp.take(candidates, chosen_slot, axis=0)  7.07 us
    select_n x2, other arithmetic, body(): packed = jnp.take(candidates, chosen_slot, axis=0)  5.63 us
  transfers between devices with their start and end apart: 3, of which 3 were waited for; matrix products, arithmetic and copies ran while one was open for 21% of the time, Pallas kernels for 0%

commit v1 on v0

--- a/solution.py
+++ b/solution.py
@@ -61,7 +61,10 @@
     block_clip = clip_ids.reshape(-1)
     token_clip = jnp.repeat(block_clip, block_rows)
     scaling = 1.0 / math.sqrt(HEAD)
-    regrouped = lax.all_to_all(grouped, "ctx", split_axis=1, concat_axis=0, tiled=True)
+    regrouped = jnp.concatenate(
+        lax.all_to_all(jnp.stack(jnp.split(grouped, lax.axis_size("ctx"), 1), axis=0), "ctx", 0, 0),
+        0,
+    )
     token_count = regrouped.shape[0]
     item_count = regrouped.shape[2]
     features = regrouped.reshape(token_count, item_count, 3 * HEAD)

time: 277 us -> 280 us (1.011)
  the two profiles are of different devices: /device:TPU:8 before, /device:TPU:16 now
where the time goes in v1:
time: 280 us
  waiting for transfers between devices  153 us (55%)
  matrix products  45.5 us (16%)
  local copies, waits for them, and re-layouts  26.2 us (9%)
  blocking collectives  18.5 us (7%)
  other arithmetic  14.7 us (5%)
  between operations  13.5 us (5%)
  starting transfers between devices  8.75 us (3%)
    ppermute x1, waiting for transfers between devices, partner(): return lax.ppermute(value, axis, pairs)  66.9 us
    all_gather x1, waiting for transfers between devices, body(): lax.all_gather(out_weight, 'dp', axis=0, tiled=True)  52.2 us
    all_to_all x1, waiting for transfers between devices, body(): lax.all_to_all(jnp.stack(jnp.split(grouped, lax.axis_size('ctx'), 1), axi...  33.1 us
    sub x4, matrix products, soft_weights(): exponent = jnp.exp(masked - row_max)  20.3 us
    dot_general x4, matrix products, one_step(): jnp.einsum('hqk,khe->qhe', weights, value_rows, preferred_element_type=jn...  19.7 us
    all_to_all x1, blocking collectives, body(): lax.all_to_all(merged, 'ctx', split_axis=0, concat_axis=1, tiled=True)  18.5 us
    unnamed x15, local copies, waits for them, and re-layouts  9.22 us
    gather x2, local copies, waits for them, and re-layouts, body(): packed = jnp.take(candidates, chosen_slot, axis=0)  7.06 us
  transfers between devices with their start and end apart: 3, of which 3 were waited for; matrix products, arithmetic and copies ran while one was open for 19% of the time, Pallas kernels for 0%

profile of v1, /device:TPU:16, one launch (start us, length us, event | category | flops | bytes accessed | tf_op | source)
XLA Modules:
  0.0 280.0 jit_solution(17478217401842957548)
XLA Ops:
  6.5 3.8 %collective-permute-start = (bf16[2,128,6144]{2,1,0:T(8,128)(2,1)}, bf16[2,128,6144]{2,1,0:T(8,128)(2,1)S(1)}, u32[]{:S(2)}, u32[]{:S(2)}) collective-permute-start(bf16[2,128,6144]{2,1,0:T(8,128)(2,1)} %bitcast.129), channel_id=1, source_target_pairs={{0,8},{8,0},{16,24},{24,16},{32,40},{40,32},{48,56},{56,48},{64,72... | collective-permute-start | bytes 9437192 | tf_op jit(solution)/shard_map/ppermute | solution.py:14
  10.4 0.7 fusion.39
  11.0 0.7 compare_and_fusion
  11.8 66.9 %collective-permute-done = bf16[2,128,6144]{2,1,0:T(8,128)(2,1)S(1)} collective-permute-done((bf16[2,128,6144]{2,1,0:T(8,128)(2,1)}, bf16[2,128,6144]{2,1,0:T(8,128)(2,1)S(1)}, u32[]{:S(2)}, u32[]{:S(2)}) %collective-permute-start) | collective-permute-done | bytes 3145760 | tf_op jit(solution)/shard_map/ppermute | solution.py:14
  78.7 5.1 %pad_maximum_fusion = bf16[4,128,6144]{2,1,0:T(8,128)(2,1)} fusion(bf16[2,128,6144]{2,1,0:T(8,128)(2,1)S(1)} %collective-permute-done, bf16[2,128,6144]{2,1,0:T(8,128)(2,1)} %bitcast.130), kind=kLoop, calls=%fused_computation.27 | loop fusion | flops 3145728 | bytes 12582912 | tf_op jit(solution)/shard_map/concatenate | solution.py:57
  83.7 3.5 %gather_fusion = bf16[2,128,6144]{2,1,0:T(8,128)(2,1)S(1)} fusion(bf16[4,128,6144]{2,1,0:T(8,128)(2,1)} %pad_maximum_fusion, s32[1024]{0:T(1024)S(1)} %pad_clamp_fusion), kind=kCustom, calls=%fused_computation | custom fusion | bytes 6291464 | tf_op jit(solution)/shard_map/jit(_take)/gather | solution.py:58
  87.3 3.5 %gather.7 = bf16[256,8,2,384]{3,2,1,0:T(2,128)(2,1)} reshape(bf16[2,128,6144]{2,1,0:T(8,128)(2,1)S(1)} %gather_fusion) | data formatting | bytes 6291456 | tf_op jit(solution)/shard_map/jit(_take)/gather | solution.py:58
  90.8 5.0 %broadcast_select_fusion = bf16[256,8,2,384]{3,2,1,0:T(2,128)(2,1)S(1)} fusion(bf16[256,8,2,384]{3,2,1,0:T(2,128)(2,1)} %gather.7, pred[256]{0:T(512)(128)(4,1)S(1)} %broadcast_bitcast_fusion.2), kind=kLoop, calls=%fused_computation.28 | loop fusion | flops 1572864 | bytes 6291712 | tf_op jit(solution)/shard_map/jit(_take)/select_n | solution.py:58
  95.8 1.0 fusion.36
  96.8 1.0 fusion.35
  97.8 1.0 fusion.34
  98.8 1.0 fusion.33
  99.8 1.0 fusion.32
  100.9 1.1 fusion.31
  101.9 1.0 fusion.30
  102.9 1.0 fusion.29
  104.0 4.9 %all-to-all-start = ((bf16[8,256,1,2,384]{4,3,1,2,0:T(2,128)(2,1)}), bf16[8,256,1,2,384]{4,3,1,2,0:T(2,128)(2,1)S(1)}, u32[]{:S(2)}, u32[]{:S(2)}) async-start(bf16[8,256,1,2,384]{4,3,1,2,0:T(2,128)(2,1)} %fusion.29), calls=%async_computation | async-start | bytes 6291456 | tf_op jit(solution)/shard_map/all_to_all | solution.py:65
  108.9 0.7 all-gather.2.cloned.1.call-update
  109.6 0.6 broadcast.219
  110.2 0.7 reduce.3
  110.9 0.1 broadcast_in_dim.47
  111.1 33.1 %all-to-all-done = bf16[8,256,1,2,384]{4,3,1,2,0:T(2,128)(2,1)S(1)} async-done(((bf16[8,256,1,2,384]{4,3,1,2,0:T(2,128)(2,1)}), bf16[8,256,1,2,384]{4,3,1,2,0:T(2,128)(2,1)S(1)}, u32[]{:S(2)}, u32[]{:S(2)}) %all-to-all-start) | async-done | bytes 3145760 | tf_op jit(solution)/shard_map/all_to_all | solution.py:65
  144.2 2.2 fusion.45
  146.4 0.1 copy.35
  146.5 0.1 copy.36
  146.6 1.1 copy.37
  147.8 46.9 %while.11 = (s32[]{:T(128)}, bf16[4,512,2,128]{3,2,1,0:T(2,128)(2,1)}, s32[4,512]{1,0:T(4,128)S(1)}, bf16[4,512,2,128]{3,1,0,2:T(8,128)(2,1)S(1)}, bf16[2048,2,1...) while((s32[]{:T(128)}, ...), condition=%wide.region_3.4_spmd.clone, body=%wide.region_0.3_spmd.clone.sunk | while | flops 1087506432 | bytes 22051484 | solution.py:43
  147.8 0.7 broadcast_compare_fusion.2
  148.5 5.1 %fusion.59 = (f32[2,512]{1,0:T(2,128)S(1)}, f32[2,512,2048]{2,1,0:T(8,128)}) fusion(pred[512,2048]{1,0:T(8,128)(4,1)S(1)} %broadcast_compare_fusion.2, bf16[2048,2,128]{2,0,1:T(8,128)(2,1)S(1)} %get-tuple-element.153, bf16[4,512,2,128]{3,1,0,2:T(8,128)(2,1)S(1)} %get-tuple-element.152, s32[]{:T(128)} %get-tuple-element.141), kind=kOutput, calls=%fused_computation.72.clone.1 | convolution fusion | flops 545261568 | bytes 10752004 | tf_op jit(solution)/shard_map/while/body/eval_jaxpr/sub | solution.py:20
  153.6 4.9 %fusion.60 = bf16[1,512,2,128]{3,1,2,0:T(8,128)(2,1)S(1)} fusion(bf16[2048,2,128]{2,0,1:T(8,128)(2,1)} %get-tuple-element.154, f32[2,512,2048]{2,1,0:T(8,128)} %get-tuple-element.131, f32[2,512]{1,0:T(2,128)S(1)} %get-tuple-element.132), kind=kOutput, calls=%fused_computation.13.clone.1 | convolution fusion | flops 541196288 | bytes 9703424 | tf_op jit(solution)/shard_map/while/body/eval_jaxpr/hqk,khe->qhe/dot_general | solution.py:39
  158.5 1.0 copy_dynamic-update-slice_fusion.2
  159.6 0.7 broadcast_compare_fusion.2
  160.3 5.1 %fusion.59 = (f32[2,512]{1,0:T(2,128)S(1)}, f32[2,512,2048]{2,1,0:T(8,128)}) fusion(pred[512,2048]{1,0:T(8,128)(4,1)S(1)} %broadcast_compare_fusion.2, bf16[2048,2,128]{2,0,1:T(8,128)(2,1)S(1)} %get-tuple-element.153, bf16[4,512,2,128]{3,1,0,2:T(8,128)(2,1)S(1)} %get-tuple-element.152, s32[]{:T(128)} %get-tuple-element.141), kind=kOutput, calls=%fused_computation.72.clone.1 | convolution fusion | flops 545261568 | bytes 10752004 | tf_op jit(solution)/shard_map/while/body/eval_jaxpr/sub | solution.py:20
  165.3 4.9 %fusion.60 = bf16[1,512,2,128]{3,1,2,0:T(8,128)(2,1)S(1)} fusion(bf16[2048,2,128]{2,0,1:T(8,128)(2,1)} %get-tuple-element.154, f32[2,512,2048]{2,1,0:T(8,128)} %get-tuple-element.131, f32[2,512]{1,0:T(2,128)S(1)} %get-tuple-element.132), kind=kOutput, calls=%fused_computation.13.clone.1 | convolution fusion | flops 541196288 | bytes 9703424 | tf_op jit(solution)/shard_map/while/body/eval_jaxpr/hqk,khe->qhe/dot_general | solution.py:39
  170.3 1.0 copy_dynamic-update-slice_fusion.2
  171.3 0.7 broadcast_compare_fusion.2
  172.0 5.1 %fusion.59 = (f32[2,512]{1,0:T(2,128)S(1)}, f32[2,512,2048]{2,1,0:T(8,128)}) fusion(pred[512,2048]{1,0:T(8,128)(4,1)S(1)} %broadcast_compare_fusion.2, bf16[2048,2,128]{2,0,1:T(8,128)(2,1)S(1)} %get-tuple-element.153, bf16[4,512,2,128]{3,1,0,2:T(8,128)(2,1)S(1)} %get-tuple-element.152, s32[]{:T(128)} %get-tuple-element.141), kind=kOutput, calls=%fused_computation.72.clone.1 | convolution fusion | flops 545261568 | bytes 10752004 | tf_op jit(solution)/shard_map/while/body/eval_jaxpr/sub | solution.py:20
  177.0 4.9 %fusion.60 = bf16[1,512,2,128]{3,1,2,0:T(8,128)(2,1)S(1)} fusion(bf16[2048,2,128]{2,0,1:T(8,128)(2,1)} %get-tuple-element.154, f32[2,512,2048]{2,1,0:T(8,128)} %get-tuple-element.131, f32[2,512]{1,0:T(2,128)S(1)} %get-tuple-element.132), kind=kOutput, calls=%fused_computation.13.clone.1 | convolution fusion | flops 541196288 | bytes 9703424 | tf_op jit(solution)/shard_map/while/body/eval_jaxpr/hqk,khe->qhe/dot_general | solution.py:39
  182.0 1.0 copy_dynamic-update-slice_fusion.2
  183.0 0.7 broadcast_compare_fusion.2
  183.7 5.1 %fusion.59 = (f32[2,512]{1,0:T(2,128)S(1)}, f32[2,512,2048]{2,1,0:T(8,128)}) fusion(pred[512,2048]{1,0:T(8,128)(4,1)S(1)} %broadcast_compare_fusion.2, bf16[2048,2,128]{2,0,1:T(8,128)(2,1)S(1)} %get-tuple-element.153, bf16[4,512,2,128]{3,1,0,2:T(8,128)(2,1)S(1)} %get-tuple-element.152, s32[]{:T(128)} %get-tuple-element.141), kind=kOutput, calls=%fused_computation.72.clone.1 | convolution fusion | flops 545261568 | bytes 10752004 | tf_op jit(solution)/shard_map/while/body/eval_jaxpr/sub | solution.py:20
  188.8 4.9 %fusion.60 = bf16[1,512,2,128]{3,1,2,0:T(8,128)(2,1)S(1)} fusion(bf16[2048,2,128]{2,0,1:T(8,128)(2,1)} %get-tuple-element.154, f32[2,512,2048]{2,1,0:T(8,128)} %get-tuple-element.131, f32[2,512]{1,0:T(2,128)S(1)} %get-tuple-element.132), kind=kOutput, calls=%fused_computation.13.clone.1 | convolution fusion | flops 541196288 | bytes 9703424 | tf_op jit(solution)/shard_map/while/body/eval_jaxpr/hqk,khe->qhe/dot_general | solution.py:39
  193.7 1.0 copy_dynamic-update-slice_fusion.2
  194.7 1.7 all_to_all.18
  196.4 18.5 %all_to_all.24 = bf16[8,256,256]{2,1,0:T(8,128)(2,1)S(1)} all-to-all(bf16[8,256,256]{2,1,0:T(8,128)(2,1)S(1)} %all_to_all.18), channel_id=1, replica_groups=mesh['dp'=64,'ctx'=8] {'ctx'}, dimensions={0} | all-to-all | bytes 2097152 | tf_op jit(solution)/shard_map/all_to_all | solution.py:76
  214.9 0.5 copy.24
  215.4 52.2 %all-gather.2.cloned.1.call-done = bf16[2048,1536]{1,0:T(8,128)(2,1)} async-done(((bf16[32,1536]{1,0:T(8,128)(2,1)}), bf16[2048,1536]{1,0:T(8,128)(2,1)}) %all-gather.2.cloned.1.call-update) | async-done | bytes 6291472 | tf_op jit(solution)/shard_map/all_gather | solution.py:79
  267.7 5.5 %convolution_convert_fusion = bf16[256,1536]{1,0:T(8,128)(2,1)} fusion(bf16[256,2048]{0,1:T(8,128)(2,1)S(1)} %bitcast.127, bf16[2048,1536]{1,0:T(8,128)(2,1)} %all-gather.2.cloned.1.call-done), kind=kOutput, calls=%fused_computation.29 | convolution fusion | flops 1611005952 | bytes 8126464 | tf_op jit(solution)/shard_map/dot_general | solution.py:77
  (16 shorter events, 0.5 us)
Async XLA Ops:
  6.5 72.1 %collective-permute-start = (bf16[2,128,6144]{2,1,0:T(8,128)(2,1)}, bf16[2,128,6144]{2,1,0:T(8,128)(2,1)S(1)}, u32[]{:S(2)}, u32[]{:S(2)}) collective-permute-start(bf16[2,128,6144]{2,1,0:T(8,128)(2,1)} %bitcast.129), channel_id=1, source_target_pairs={{0,8},{8,0},{16,24},{24,16},{32,40},{40,32},{48,56},{56,48},{64,72... | collective-permute-start | bytes 9437192 | tf_op jit(solution)/shard_map/ppermute | solution.py:14
  104.0 6.3 %copy-start = (s32[1,16]{1,0:T(1,128)S(1)}, s32[1,16]{1,0:T(1,128)}, u32[]{:S(2)}) copy-start(s32[1,16]{1,0:T(1,128)} %param.8) | copy-start | bytes 196
  104.0 40.2 %all-to-all-start = ((bf16[8,256,1,2,384]{4,3,1,2,0:T(2,128)(2,1)}), bf16[8,256,1,2,384]{4,3,1,2,0:T(2,128)(2,1)S(1)}, u32[]{:S(2)}, u32[]{:S(2)}) async-start(bf16[8,256,1,2,384]{4,3,1,2,0:T(2,128)(2,1)} %fusion.29), calls=%async_computation | async-start | bytes 6291456 | tf_op jit(solution)/shard_map/all_to_all | solution.py:65
  108.9 158.8 %all-gather.2.cloned.1.call-start = ((), (), s32[]{:S(2)}) async-start(), calls=%async_computation.2 | async-start | bytes 6389760 | tf_op jit(solution)/shard_map/all_gather | solution.py:79
Sparse Core Ops, SparseCore 0:
  112.6 154.9 all-gather.1
